TPU v7x, 256 devices: a whole 4x4x8 slice. The times are simulated.
256 devices in a mesh: tm: 16 (over y, x), tile: 16 (over z, core).
Axes of the slice: x: 4, y: 4, z: 8, core: 2. Of those that a mesh axis runs over, the one named last changes fastest.
Arguments:
- latent: bfloat16 [64, 64, 32, 256], P('tm', 'tile'), may hold values from -6 to 6
- tile_rows: int32 [16], replicated, may hold values from 1 to 4, 32 in all
- kernel_one: bfloat16 [3, 3, 3, 256, 256], replicated, may hold values from -0.078125 to 0.078125
- bias_one: float32 [256], replicated, may hold values from -3 to 3
- kernel_two: bfloat16 [3, 3, 3, 256, 256], replicated, may hold values from -0.078125 to 0.078125
- bias_two: float32 [256], replicated, may hold values from -3 to 3
Outputs:
- frames_out: bfloat16 [64, 128, 64, 256], P('tm', 'tile')
Inputs may be any that keep to these rules, and one draw needn't show every extreme that they name: `tile_rows`: each tile has 1 to 4 rows, they sum to 32, and some tile has exactly 4.
All inputs are finite; a program needn't handle non-finite values.
Results may differ from a plain program's by a relative error of at most 0.0031.
Values may be sent and summed in bfloat16 or wider, within the bound.
A program may use at most 64 MiB of HBM per device.

v0:
```python
import jax
import jax.numpy as jnp
from jax import lax
from jax.sharding import PartitionSpec as P


def padded(block, sides, width):
    for axis, dim in sides:
        count = lax.axis_size(axis)
        forward = [(i, i + 1) for i in range(count - 1)]
        backward = [(target, source) for source, target in forward]
        low = lax.ppermute(
            lax.slice_in_dim(block, block.shape[dim] - width, None, axis=dim), axis, forward
        )
        high = lax.ppermute(lax.slice_in_dim(block, 0, width, axis=dim), axis, backward)
        block = jnp.concatenate([low, block, high], axis=dim)
    return block


def passed_along(block, axis, distance):
    devices = range(lax.axis_size(axis))
    route = [(i - distance, i) for i in devices if i - distance in devices]
    return lax.ppermute(block, axis, route)


def upsample(field):
    return jnp.repeat(jnp.repeat(field, 2, axis=1), 2, axis=2)


def edge_pair(field, last):
    tail = lax.dynamic_slice_in_dim(field, last, 1, axis=1)
    return jnp.concatenate([field[:, 0:1], tail], axis=1)


def attach(field, above, below, place):
    extended = jnp.concatenate([above, field, jnp.zeros_like(above)], axis=1)
    row_ids = jnp.arange(extended.shape[1], dtype=jnp.int32)
    return jnp.where((row_ids == place)[None, :, None, None], below, extended)


def convolve(field, kernel, bias):
    result = lax.conv_general_dilated(
        field[None],
        kernel,
        (1, 1, 1),
        ((0, 0), (0, 0), (1, 1)),
        dimension_numbers=("NDHWC", "DHWIO", "NDHWC"),
        preferred_element_type=jnp.float32,
    )
    return result[0] + bias


def local(latent, tile_rows, kernel_one, bias_one, kernel_two, bias_two):
    frames = latent.shape[0]
    cap = latent.shape[1]
    tile_pos = lax.axis_index("tile")
    length = lax.dynamic_slice_in_dim(tile_rows, tile_pos, 1)[0]
    first_group = lax.axis_index("tm") == 0
    valid = jnp.arange(cap, dtype=jnp.int32) < length
    clean = jnp.where(valid[None, :, None, None], latent, 0)
    rimmed = padded(edge_pair(clean, length - 1), (("tile", 1),), 1)
    lat_ext = attach(clean, rimmed[:, 0:1], rimmed[:, 3:4], length + 1)
    residual = upsample(clean).astype(jnp.float32)
    earlier = passed_along(lat_ext[frames - 2 :], "tm", 1)
    earlier = jnp.where(first_group, jnp.broadcast_to(lat_ext[0:1], earlier.shape), earlier)
    source = upsample(jnp.concatenate([earlier, lat_ext], axis=0))[:, 1 : 2 * cap + 3]
    act_one = convolve(source, kernel_one, bias_one)
    keep = jnp.arange(2 * cap, dtype=jnp.int32) < 2 * length
    hidden = jnp.where(keep[None, :, None, None], jax.nn.silu(act_one), 0.0).astype(jnp.bfloat16)
    rimmed_hidden = padded(edge_pair(hidden, 2 * length - 1), (("tile", 1),), 1)
    own = attach(hidden, rimmed_hidden[:, 0:1], rimmed_hidden[:, 3:4], 2 * length + 1)
    before = passed_along(own[frames - 2 :], "tm", 1)
    before = jnp.where(first_group, jnp.broadcast_to(own[0:1], before.shape), before)
    hid_ext = jnp.concatenate([before, own], axis=0)
    act_two = convolve(hid_ext, kernel_two, bias_two)
    out_keep = jnp.arange(2 * cap, dtype=jnp.int32) < 2 * length
    return jnp.where(out_keep[None, :, None, None], act_two + residual, 0.0).astype(jnp.bfloat16)


def solution(mesh):
    in_specs = (P("tm", "tile", None, None), P(), P(), P(), P(), P())
    out_specs = P("tm", "tile", None, None)
    return jax.shard_map(local, mesh=mesh, in_specs=in_specs, out_specs=out_specs, check_vma=False)
```

profile of v0, /device:TPU:112, one launch (start us, length us, event | category | flops | bytes accessed | tf_op | source)
XLA Modules:
  0.0 94.5 jit_solution(378032308903884088)
XLA Ops:
  0.0 1.4 %dynamic_slice.9 = s32[1]{0:T(128)} dynamic-slice(s32[16]{0:T(128)} %param.7, s32[]{:T(128)S(6)} %select_n.44), dynamic_slice_sizes={1} | dynamic-slice | bytes 12 | tf_op jit(solution)/shard_map/dynamic_slice | solution.py:57
  5.7 1.9 %collective-permute-start = (bf16[4,1,32,256]{3,2,1,0:T(8,128)(2,1)}, bf16[4,1,32,256]{3,2,1,0:T(8,128)(2,1)}, u32[]{:S(2)}, u32[]{:S(2)}) collective-permute-start(bf16[4,1,32,256]{3,2,1,0:T(8,128)(2,1)} %get-tuple-element.7), channel_id=1, source_target_pairs={{1,0},{2,1},{3,2},{4,3},{5,4},{6,5},{7,6},{8,7},{9,8},{10,9},{11,1... | collective-permute-start | bytes 196616 | tf_op jit(solution)/shard_map/ppermute | solution.py:15
  7.6 2.4 %collective-permute-start.1 = (bf16[4,1,32,256]{3,2,1,0:T(8,128)(2,1)}, bf16[4,1,32,256]{3,2,1,0:T(8,128)(2,1)}, u32[]{:S(2)}, u32[]{:S(2)}) collective-permute-start(bf16[4,1,32,256]{3,2,1,0:T(8,128)(2,1)} %get-tuple-element.8), channel_id=1, source_target_pairs={{0,1},{1,2},{2,3},{3,4},{4,5},{5,6},{6,7},{7,8},{8,9},{9,10},{10,1... | collective-permute-start | bytes 196616 | tf_op jit(solution)/shard_map/ppermute | solution.py:12
  11.3 2.2 %collective-permute-done.1 = bf16[4,1,32,256]{3,2,1,0:T(8,128)(2,1)} collective-permute-done((bf16[4,1,32,256]{3,2,1,0:T(8,128)(2,1)}, bf16[4,1,32,256]{3,2,1,0:T(8,128)(2,1)}, u32[]{:S(2)}, u32[]{:S(2)}) %collective-permute-start.1) | collective-permute-done | bytes 65568 | tf_op jit(solution)/shard_map/ppermute | solution.py:12
  13.5 1.1 %maximum_select_fusion.1 = bf16[4,6,32,256]{3,2,1,0:T(8,128)(2,1)S(1)} fusion(bf16[4,4,32,256]{3,2,1,0:T(8,128)(2,1)} %copy-done.5, bf16[4,1,32,256]{3,2,1,0:T(8,128)(2,1)} %collective-permute-done.1, pred[6]{0:T(512)(128)(4,1)S(1)} %iota_compare_fusion.2, bf16[6]{0:T(256)(128)(2,1)S(1)} %pad.17.clone, bf16[4,32,256]{2,1,0:T(8,128)(2,1)} %bitcast.1), kind=kLoop, calls=%fused_computation.33 | loop fusion | flops 589824 | bytes 786450 | tf_op jit(solution)/shard_map/jit(_where)/select_n | solution.py:38
  14.6 3.4 %collective-permute-start.2 = (bf16[2,6,32,256]{3,2,1,0:T(8,128)(2,1)S(1)}, bf16[2,6,32,256]{3,2,1,0:T(8,128)(2,1)S(1)}, u32[]{:S(2)}, u32[]{:S(2)}) collective-permute-start(bf16[2,6,32,256]{3,2,1,0:T(8,128)(2,1)S(1)} %slice.34), channel_id=1, source_target_pairs={{0,16},{16,32},{32,48},{48,64},{64,80},{80,96},{96,112},{112,128},... | collective-permute-start | bytes 589832 | tf_op jit(solution)/shard_map/ppermute | solution.py:23
  18.0 8.3 %collective-permute-done.2 = bf16[2,6,32,256]{3,2,1,0:T(8,128)(2,1)S(1)} collective-permute-done((bf16[2,6,32,256]{3,2,1,0:T(8,128)(2,1)S(1)}, bf16[2,6,32,256]{3,2,1,0:T(8,128)(2,1)S(1)}, u32[]{:S(2)}, u32[]{:S(2)}) %collective-permute-start.2) | collective-permute-done | bytes 196640 | tf_op jit(solution)/shard_map/ppermute | solution.py:23
  28.5 9.0 %fusion.24 = f32[4,8,8,9,256]{4,2,3,1,0:T(8,128)S(1)} fusion(bf16[3,3,3,256,256]{4,3,2,1,0:T(8,128)(2,1)S(1)} %copy-done, bf16[6,10,1,7,2,256]{5,3,4,1,0,2:T(8,128)(2,1)S(1)} %slice.36, bf16[6,10,1,8,9,256]{5,3,4,1,0,2:T(8,128)(2,1)S(1)} %copy.29, pred[8,9]{0,1:T(8,128)(4,1)S(1)} %copy-done.10), kind=kOutput, calls=%fused_computation.27 | convolution fusion | flops 8162426880 | bytes 8540232 | tf_op jit(solution)/shard_map/conv_general_dilated | solution.py:42
  40.1 1.2 %fusion.35 = (bf16[4,1,64,256]{3,1,2,0:T(2,128)(2,1)}, bf16[4,1,64,256]{3,1,2,0:T(2,128)(2,1)}) fusion(bf16[4,8,64,256]{3,1,2,0:T(8,128)(2,1)S(1)} %select_convert_fusion, s32[]{:T(128)S(6)} %select_n.52), kind=kLoop, calls=%fused_computation.50 | loop fusion | bytes 524292 | tf_op jit(solution)/shard_map/slice | solution.py:32
  41.3 1.9 %collective-permute-start.3 = (bf16[4,1,64,256]{3,1,2,0:T(2,128)(2,1)}, bf16[4,1,64,256]{3,1,2,0:T(2,128)(2,1)}, u32[]{:S(2)}, u32[]{:S(2)}) collective-permute-start(bf16[4,1,64,256]{3,1,2,0:T(2,128)(2,1)} %get-tuple-element.5), channel_id=1, source_target_pairs={{1,0},{2,1},{3,2},{4,3},{5,4},{6,5},{7,6},{8,7},{9,8},{10,9},{11,1... | collective-permute-start | bytes 393224 | tf_op jit(solution)/shard_map/ppermute | solution.py:15
  43.2 2.4 %collective-permute-start.4 = (bf16[4,1,64,256]{3,1,2,0:T(2,128)(2,1)}, bf16[4,1,64,256]{3,1,2,0:T(2,128)(2,1)}, u32[]{:S(2)}, u32[]{:S(2)}) collective-permute-start(bf16[4,1,64,256]{3,1,2,0:T(2,128)(2,1)} %get-tuple-element.6), channel_id=1, source_target_pairs={{0,1},{1,2},{2,3},{3,4},{4,5},{5,6},{6,7},{7,8},{8,9},{9,10},{10,1... | collective-permute-start | bytes 393224 | tf_op jit(solution)/shard_map/ppermute | solution.py:12
  45.7 1.7 %collective-permute-done.3 = bf16[4,1,64,256]{3,1,2,0:T(2,128)(2,1)} collective-permute-done((bf16[4,1,64,256]{3,1,2,0:T(2,128)(2,1)}, bf16[4,1,64,256]{3,1,2,0:T(2,128)(2,1)}, u32[]{:S(2)}, u32[]{:S(2)}) %collective-permute-start.3) | collective-permute-done | bytes 131104 | tf_op jit(solution)/shard_map/ppermute | solution.py:15
  48.3 2.9 %collective-permute-done.4 = bf16[4,1,64,256]{3,1,2,0:T(2,128)(2,1)} collective-permute-done((bf16[4,1,64,256]{3,1,2,0:T(2,128)(2,1)}, bf16[4,1,64,256]{3,1,2,0:T(2,128)(2,1)}, u32[]{:S(2)}, u32[]{:S(2)}) %collective-permute-start.4) | collective-permute-done | bytes 131104 | tf_op jit(solution)/shard_map/ppermute | solution.py:12
  51.2 2.7 %maximum_select_fusion = bf16[4,10,64,256]{3,1,2,0:T(8,128)(2,1)S(1)} fusion(bf16[4,8,64,256]{3,1,2,0:T(8,128)(2,1)} %copy-done.3, bf16[4,1,64,256]{3,1,2,0:T(2,128)(2,1)} %collective-permute-done.4, pred[10]{0:T(512)(128)(4,1)S(1)} %iota_compare_fusion.3, bf16[10]{0:T(256)(128)(2,1)S(1)} %pad.10.clone, bf16[4,64,256]{2,1,0:T(8,128)(2,1)S(1)} %bitcast.59), kind=kLoop, calls=%fused_computation.24 | loop fusion | flops 4587520 | bytes 2621470 | tf_op jit(solution)/shard_map/jit(_where)/select_n | solution.py:38
  53.9 1.3 %copy-done.1 = bf16[4,10,64,256]{3,1,2,0:T(8,128)(2,1)} copy-done((bf16[4,10,64,256]{3,1,2,0:T(8,128)(2,1)}, bf16[4,10,64,256]{3,1,2,0:T(8,128)(2,1)S(1)}, u32[]{:S(2)}) %copy-start.1) | copy-done | bytes 1310744
  55.3 1.1 %copy.31 = bf16[2,10,64,256]{3,2,1,0:T(8,128)(2,1)} copy(bf16[2,10,64,256]{3,1,2,0:T(8,128)(2,1)S(1)} %slice.40) | data formatting | bytes 1310720 | tf_op jit(solution)/shard_map/slice | solution.py:72
  56.4 1.9 %collective-permute-start.5 = (bf16[2,10,64,256]{3,2,1,0:T(8,128)(2,1)}, bf16[2,10,64,256]{3,2,1,0:T(8,128)(2,1)}, u32[]{:S(2)}, u32[]{:S(2)}) collective-permute-start(bf16[2,10,64,256]{3,2,1,0:T(8,128)(2,1)} %copy.31), channel_id=1, source_target_pairs={{0,16},{16,32},{32,48},{48,64},{64,80},{80,96},{96,112},{112,128},... | collective-permute-start | bytes 1966088 | tf_op jit(solution)/shard_map/ppermute | solution.py:23
  58.5 1.3 %broadcast_in_dim.129 = f32[4,4,2,32,256]{4,2,1,3,0:T(2,128)} broadcast(f32[4,4,32,256]{3,1,2,0:T(4,128)S(1)} %copy.37), dimensions={0,1,3,4} | broadcast | bytes 1572864 | tf_op jit(solution)/shard_map/broadcast_in_dim | solution.py:27
  59.9 2.9 %convert_element_type.21 = f32[4,8,32,256]{3,1,2,0:T(8,128)} reshape(f32[4,4,2,32,256]{4,2,1,3,0:T(2,128)} %broadcast_in_dim.129) | data formatting | bytes 2097152 | tf_op jit(solution)/shard_map/convert_element_type | solution.py:63
  62.8 1.2 %slice_bitcast_fusion.3 = bf16[10,64,256]{2,0,1:T(8,128)(2,1)S(1)} fusion(bf16[4,10,64,256]{3,1,2,0:T(8,128)(2,1)} %copy-done.1), kind=kLoop, calls=%fused_computation.32 | loop fusion | bytes 655360 | tf_op jit(solution)/shard_map/broadcast_in_dim | solution.py:73
  64.0 13.8 %collective-permute-done.5 = bf16[2,10,64,256]{3,2,1,0:T(8,128)(2,1)} collective-permute-done((bf16[2,10,64,256]{3,2,1,0:T(8,128)(2,1)}, bf16[2,10,64,256]{3,2,1,0:T(8,128)(2,1)}, u32[]{:S(2)}, u32[]{:S(2)}) %collective-permute-start.5) | collective-permute-done | bytes 655392 | tf_op jit(solution)/shard_map/ppermute | solution.py:23
  77.8 1.5 %copy_select_fusion = bf16[2,10,64,256]{3,1,2,0:T(8,128)(2,1)S(1)} fusion(bf16[2,10,64,256]{3,2,1,0:T(8,128)(2,1)} %collective-permute-done.5, pred[]{:T(512)S(6)} %eq.23, bf16[10,64,256]{2,0,1:T(8,128)(2,1)S(1)} %slice_bitcast_fusion.3), kind=kLoop, calls=%fused_computation.30 | loop fusion | flops 327680 | bytes 1638401 | tf_op jit(solution)/shard_map/jit(_where)/select_n | solution.py:73
  82.2 9.1 %fusion.21 = f32[4,8,8,9,256]{4,2,3,1,0:T(8,128)S(1)} fusion(bf16[3,3,3,256,256]{4,3,2,1,0:T(8,128)(2,1)S(1)} %copy-done.9, bf16[6,10,1,7,2,256]{5,3,4,1,0,2:T(8,128)(2,1)S(1)} %slice.41, bf16[6,10,1,8,9,256]{5,3,4,1,0,2:T(8,128)(2,1)S(1)} %copy.35, pred[8,9]{0,1:T(8,128)(4,1)S(1)} %copy-done.10), kind=kOutput, calls=%fused_computation.26 | convolution fusion | flops 8162426880 | bytes 8540232 | tf_op jit(solution)/shard_map/conv_general_dilated | solution.py:42
  93.3 1.2 %copy.38 = bf16[4,8,64,256]{3,2,1,0:T(8,128)(2,1)} copy(bf16[4,8,64,256]{3,1,2,0:T(8,128)(2,1)S(1)} %fusion.19) | data formatting | bytes 2097152 | tf_op jit(solution)/shard_map/convert_element_type | solution.py:77
  (53 shorter events, 13.9 us)
Async XLA Ops:
  0.0 28.4 %copy-start = (bf16[3,3,3,256,256]{4,3,2,1,0:T(8,128)(2,1)S(1)}, bf16[3,3,3,256,256]{4,3,2,1,0:T(8,128)(2,1)}, u32[]{:S(2)}) copy-start(bf16[3,3,3,256,256]{4,3,2,1,0:T(8,128)(2,1)} %param.8) | copy-start | bytes 10616836
  4.3 0.7 copy-start.5
  5.7 5.7 %collective-permute-start = (bf16[4,1,32,256]{3,2,1,0:T(8,128)(2,1)}, bf16[4,1,32,256]{3,2,1,0:T(8,128)(2,1)}, u32[]{:S(2)}, u32[]{:S(2)}) collective-permute-start(bf16[4,1,32,256]{3,2,1,0:T(8,128)(2,1)} %get-tuple-element.7), channel_id=1, source_target_pairs={{1,0},{2,1},{3,2},{4,3},{5,4},{6,5},{7,6},{8,7},{9,8},{10,9},{11,1... | collective-permute-start | bytes 196616 | tf_op jit(solution)/shard_map/ppermute | solution.py:15
  7.6 5.9 %collective-permute-start.1 = (bf16[4,1,32,256]{3,2,1,0:T(8,128)(2,1)}, bf16[4,1,32,256]{3,2,1,0:T(8,128)(2,1)}, u32[]{:S(2)}, u32[]{:S(2)}) collective-permute-start(bf16[4,1,32,256]{3,2,1,0:T(8,128)(2,1)} %get-tuple-element.8), channel_id=1, source_target_pairs={{0,1},{1,2},{2,3},{3,4},{4,5},{5,6},{6,7},{7,8},{8,9},{9,10},{10,1... | collective-permute-start | bytes 196616 | tf_op jit(solution)/shard_map/ppermute | solution.py:12
  14.6 11.7 %collective-permute-start.2 = (bf16[2,6,32,256]{3,2,1,0:T(8,128)(2,1)S(1)}, bf16[2,6,32,256]{3,2,1,0:T(8,128)(2,1)S(1)}, u32[]{:S(2)}, u32[]{:S(2)}) collective-permute-start(bf16[2,6,32,256]{3,2,1,0:T(8,128)(2,1)S(1)} %slice.34), channel_id=1, source_target_pairs={{0,16},{16,32},{32,48},{48,64},{64,80},{80,96},{96,112},{112,128},... | collective-permute-start | bytes 589832 | tf_op jit(solution)/shard_map/ppermute | solution.py:23
  27.8 0.7 copy-start.10
  37.5 0.7 copy-start.7
  39.1 1.0 %copy-start.3 = (bf16[4,8,64,256]{3,1,2,0:T(8,128)(2,1)}, bf16[4,8,64,256]{3,1,2,0:T(8,128)(2,1)S(1)}, u32[]{:S(2)}) copy-start(bf16[4,8,64,256]{3,1,2,0:T(8,128)(2,1)S(1)} %select_convert_fusion) | copy-start | bytes 3145732
  41.3 6.1 %collective-permute-start.3 = (bf16[4,1,64,256]{3,1,2,0:T(2,128)(2,1)}, bf16[4,1,64,256]{3,1,2,0:T(2,128)(2,1)}, u32[]{:S(2)}, u32[]{:S(2)}) collective-permute-start(bf16[4,1,64,256]{3,1,2,0:T(2,128)(2,1)} %get-tuple-element.5), channel_id=1, source_target_pairs={{1,0},{2,1},{3,2},{4,3},{5,4},{6,5},{7,6},{8,7},{9,8},{10,9},{11,1... | collective-permute-start | bytes 393224 | tf_op jit(solution)/shard_map/ppermute | solution.py:15
  43.2 8.0 %collective-permute-start.4 = (bf16[4,1,64,256]{3,1,2,0:T(2,128)(2,1)}, bf16[4,1,64,256]{3,1,2,0:T(2,128)(2,1)}, u32[]{:S(2)}, u32[]{:S(2)}) collective-permute-start(bf16[4,1,64,256]{3,1,2,0:T(2,128)(2,1)} %get-tuple-element.6), channel_id=1, source_target_pairs={{0,1},{1,2},{2,3},{3,4},{4,5},{5,6},{6,7},{7,8},{8,9},{9,10},{10,1... | collective-permute-start | bytes 393224 | tf_op jit(solution)/shard_map/ppermute | solution.py:12
  53.9 1.3 %copy-start.1 = (bf16[4,10,64,256]{3,1,2,0:T(8,128)(2,1)}, bf16[4,10,64,256]{3,1,2,0:T(8,128)(2,1)S(1)}, u32[]{:S(2)}) copy-start(bf16[4,10,64,256]{3,1,2,0:T(8,128)(2,1)S(1)} %maximum_select_fusion) | copy-start | bytes 3932164
  55.3 3.0 %copy-start.6 = (bf16[4,4,32,256]{3,2,1,0:T(8,128)(2,1)S(1)}, bf16[4,4,32,256]{3,2,1,0:T(8,128)(2,1)}, u32[]{:S(2)}) copy-start(bf16[4,4,32,256]{3,2,1,0:T(8,128)(2,1)} %copy-done.5) | copy-start | bytes 786436
  56.4 21.4 %collective-permute-start.5 = (bf16[2,10,64,256]{3,2,1,0:T(8,128)(2,1)}, bf16[2,10,64,256]{3,2,1,0:T(8,128)(2,1)}, u32[]{:S(2)}, u32[]{:S(2)}) collective-permute-start(bf16[2,10,64,256]{3,2,1,0:T(8,128)(2,1)} %copy.31), channel_id=1, source_target_pairs={{0,16},{16,32},{32,48},{48,64},{64,80},{80,96},{96,112},{112,128},... | collective-permute-start | bytes 1966088 | tf_op jit(solution)/shard_map/ppermute | solution.py:23
  62.8 16.6 %copy-start.2 = (bf16[4,10,64,256]{3,1,2,0:T(8,128)(2,1)S(1)}, bf16[4,10,64,256]{3,1,2,0:T(8,128)(2,1)}, u32[]{:S(2)}) copy-start(bf16[4,10,64,256]{3,1,2,0:T(8,128)(2,1)} %copy-done.1) | copy-start | bytes 3932164
  80.2 2.0 %copy-start.9 = (bf16[3,3,3,256,256]{4,3,2,1,0:T(8,128)(2,1)S(1)}, bf16[3,3,3,256,256]{4,3,2,1,0:T(8,128)(2,1)}, u32[]{:S(2)}) copy-start(bf16[3,3,3,256,256]{4,3,2,1,0:T(8,128)(2,1)} %param.10) | copy-start | bytes 10616836
  91.3 1.2 %copy-start.4 = (f32[4,8,32,256]{3,1,2,0:T(8,128)S(1)}, f32[4,8,32,256]{3,1,2,0:T(8,128)}, u32[]{:S(2)}) copy-start(f32[4,8,32,256]{3,1,2,0:T(8,128)} %convert_element_type.21) | copy-start | bytes 3145732
  92.0 0.8 copy-start.8
where the time goes:
time: 95.1 us; the launch traced here: 94.5 us
  waiting for transfers between devices  28.8 us (30%)
  local copies, waits for them, and re-layouts  22.2 us (23%)
  matrix products  18.1 us (19%)
  starting transfers between devices  13.9 us (15%)
  other arithmetic  8.73 us (9%)
  between operations  2.8 us (3%)
    ppermute x2, waiting for transfers between devices, passed_along(): return lax.ppermute(block, axis, route)  22.1 us
    conv_general_dilated x2, matrix products, convolve(): lax.conv_general_dilated(field[None], kernel, (1, 1, 1), ((0, 0), (0, 0),...  18.1 us
    unnamed x23, local copies, waits for them, and re-layouts  5.65 us
    ppermute x2, starting transfers between devices, passed_along(): return lax.ppermute(block, axis, route)  5.31 us
    ppermute x2, waiting for transfers between devices, padded(): lax.ppermute(lax.slice_in_dim(block, block.shape[dim] - width, None, axis...  5.01 us
    ppermute x2, starting transfers between devices, padded(): lax.ppermute(lax.slice_in_dim(block, block.shape[dim] - width, None, axis...  4.81 us
    ppermute x2, starting transfers between devices, padded(): lax.ppermute(lax.slice_in_dim(block, 0, width, axis=dim), axis, backward)  3.82 us
    select_n x2, other arithmetic, attach(): return jnp.where((row_ids == place)[None, :, None, None], below, extended)  3.78 us
  transfers between devices with their start and end apart: 6, of which 5 were waited for; matrix products, arithmetic and copies ran while one was open for 7% of the time, Pallas kernels for 0%

commit v1 on v0

v1 whole, which is shorter than its diff:
```python
import functools

import jax
import jax.numpy as jnp
from jax import lax
from jax.experimental import pallas as pl
from jax.experimental.pallas import tpu as pltpu
from jax.sharding import PartitionSpec as P

MESH = pl.DeviceIdType.MESH
F32, BF16 = jnp.float32, jnp.bfloat16


def shifted(value, by, cols, keep):
    return jnp.where(keep, pltpu.roll(value, by % value.shape[0], axis=0), 0.0)


def spread(ext, hid, k, w1, half_bias, first, last, length, dims):
    cap, cols, ch = dims
    n = (cap + 1) * cols
    taps = jnp.concatenate([ext[k], ext[k + 1], ext[k + 2]], axis=1)
    upper, lower = taps[:n], taps[cols:]
    ends = jnp.concatenate([upper, lower], axis=1)
    side = lax.broadcasted_iota(jnp.int32, (n, ch), 0) % cols
    after_first, before_last = side != 0, side != cols - 1
    even_rows, odd_rows = [], []
    for q in range(3):
        outer = jnp.concatenate([w1[:, 0, q].reshape(3 * ch, ch), w1[:, 2, q].reshape(3 * ch, ch)], axis=0)
        shared = jnp.dot(ends, outer, preferred_element_type=F32)
        centre = jnp.dot(taps, w1[:, 1, q].reshape(3 * ch, ch), preferred_element_type=F32)
        even_rows.append(shared + centre[cols:])
        odd_rows.append(shared + centre[:n])
    slot = lax.broadcasted_iota(jnp.int32, (n, ch), 0) // cols
    keep_odd = jnp.logical_or(slot > 0, first == 0)
    keep_even = jnp.logical_or(slot != length, last == 0)
    for parity, (z, keep) in enumerate([(odd_rows, keep_odd), (even_rows, keep_even)]):
        even = shifted(z[0], 1, cols, after_first) + (z[1] + z[2])
        odd = (z[0] + z[1]) + shifted(z[2], -1, cols, before_last)
        pair = []
        for v in (even, odd):
            h = v * 0.5 + half_bias
            h = h + h * jnp.tanh(h)
            pair.append(jnp.where(keep, h, 0.0))
        even, odd = pair
        four = [shifted(odd, 1, cols, after_first), even, odd, shifted(even, -1, cols, before_last)]
        for variant, v in enumerate(four):
            hid[k, variant, :, parity] = v.astype(BF16).reshape(cap + 1, cols, ch)


def gather_taps(hid, f, w2, dims):
    cap, cols, ch = dims
    total = None
    for a in range(3):
        for p in range(3):
            for q in range(3):
                rows = hid[f + a, q : q + 2].reshape(2, 2 * cap + 2, cols, ch)[:, p : p + 2 * cap]
                part = jnp.dot(rows.reshape(4 * cap * cols, ch), w2[a, p, q], preferred_element_type=F32)
                total = part if total is None else total + part
    return total


def finish(total, ext, f, stage, slot, bias, length, frames, dims):
    cap, cols, ch = dims
    total = (total + bias).reshape(2, 2 * cap, cols, ch)
    residual = ext[frames + f, cols : (cap + 1) * cols].astype(F32).reshape(cap, 1, cols, ch)
    residual = jnp.broadcast_to(residual, (cap, 2, cols, ch)).reshape(2 * cap, cols, ch)
    row = lax.broadcasted_iota(jnp.int32, (2 * cap, cols, ch), 0)
    pair = [jnp.where(row < 2 * length, total[c] + residual, 0.0) for c in range(2)]
    stage[slot] = jnp.stack(pair, axis=2).reshape(2 * cap, 2 * cols, ch).astype(BF16)


def extend(raw, ext, k, length, dims):
    cap, cols, ch = dims
    below = raw[k, cap + 1]
    for j in range(cap + 2):
        value = raw[k, j]
        if 2 <= j <= cap:
            value = jnp.where(length + 1 == j, below, value)
        ext[k, j * cols : (j + 1) * cols] = value


def block_kernel(counts, comm, tile_rows, lat, w1_hbm, b1, w2_hbm, b2, out, raw, ext, hid, w1, w2, rim, stage,
                 load_sem, out_sem, rim_send, rim_recv, main_send, main_recv):
    n_tm, n_tile = counts
    frames, cap, cols, ch = lat.shape
    dims = (cap, cols, ch)
    group = lax.axis_index("tm") if comm else jnp.int32(0)
    tile = lax.axis_index("tile") if comm else jnp.int32(5)
    length = tile_rows[tile]
    first, last = (tile == 0).astype(jnp.int32), (tile == n_tile - 1).astype(jnp.int32)
    has_up, has_down = tile > 0, tile < n_tile - 1
    has_next, has_prev = group < n_tm - 1, group > 0

    own = pltpu.make_async_copy(lat, raw.at[frames : 2 * frames, 1 : cap + 1], load_sem.at[0])
    own.start()
    load_one = pltpu.make_async_copy(w1_hbm, w1, load_sem.at[1])
    load_one.start()
    load_two = pltpu.make_async_copy(w2_hbm, w2, load_sem.at[2])
    load_two.start()

    sides = [(0, -1), (0, 1)]
    onward = [(1, 0), (1, -1), (1, 1)]

    def exists(dg, dt):
        ok = jnp.bool_(True)
        if dg > 0:
            ok = jnp.logical_and(ok, has_next)
        if dg < 0:
            ok = jnp.logical_and(ok, has_prev)
        if dt > 0:
            ok = jnp.logical_and(ok, has_down)
        if dt < 0:
            ok = jnp.logical_and(ok, has_up)
        return ok

    def device(dg, dt):
        return (group + dg, tile + dt)

    own.wait()
    for f in range(frames):
        rim[f] = raw[frames + f, length]

    def side_copy(i):
        dt = sides[i][1]
        source = raw.at[frames : 2 * frames, 1] if dt < 0 else rim
        place = cap + 1 if dt < 0 else 0
        return pltpu.make_async_remote_copy(
            src_ref=source, dst_ref=raw.at[frames : 2 * frames, place],
            send_sem=rim_send.at[i], recv_sem=rim_recv.at[i],
            device_id=device(*sides[i]), device_id_type=MESH)

    def onward_copy(i, f):
        dt = onward[i][1]
        if dt == 0:
            source, target = raw.at[frames + f, 1 : cap + 1], raw.at[f, 1 : cap + 1]
        elif dt < 0:
            source, target = raw.at[frames + f, 1], raw.at[f, cap + 1]
        else:
            source, target = rim.at[f], raw.at[f, 0]
        return pltpu.make_async_remote_copy(
            src_ref=source, dst_ref=target,
            send_sem=main_send.at[i, f], recv_sem=main_recv.at[i, f],
            device_id=device(*onward[i]), device_id_type=MESH)

    if comm:
        barrier = pltpu.get_barrier_semaphore()
        for dg, dt in sides + onward:
            @pl.when(exists(-dg, -dt))
            def _():
                pl.semaphore_signal(barrier, inc=1, device_id=device(-dg, -dt), device_id_type=MESH)
        peers = sum(exists(dg, dt).astype(jnp.int32) for dg, dt in sides + onward)
        pl.semaphore_wait(barrier, peers)
        for i in range(2):
            @pl.when(exists(*sides[i]))
            def _():
                side_copy(i).start()
        for f in reversed(range(frames)):
            for i in range(3):
                @pl.when(exists(*onward[i]))
                def _():
                    onward_copy(i, f).start()

    @pl.when(jnp.logical_not(has_up))
    def _():
        for k in range(2 * frames):
            raw[k, 0] = jnp.zeros((cols, ch), BF16)

    @pl.when(jnp.logical_not(has_down))
    def _():
        for k in range(2 * frames):
            raw[k, cap + 1] = jnp.zeros((cols, ch), BF16)

    if comm:
        for i in range(2):
            @pl.when(exists(0, -sides[i][1]))
            def _():
                side_copy(i).wait_recv()
    for k in range(frames, 2 * frames):
        extend(raw, ext, k, length, dims)

    half_bias = b1[...] * 0.5
    args = (w1, half_bias, first, last, length, dims)
    load_one.wait()
    spread(ext, hid, frames + 1, *args)
    spread(ext, hid, frames, *args)
    load_two.wait()
    for f in reversed(range(frames)):
        if comm:
            for i in range(3):
                @pl.when(exists(-onward[i][0], -onward[i][1]))
                def _():
                    onward_copy(i, f).wait_recv()

        @pl.when(has_prev)
        def _():
            extend(raw, ext, f, length, dims)

        @pl.when(jnp.logical_not(has_prev))
        def _():
            ext[f] = ext[frames]

        spread(ext, hid, f, *args)
        total = gather_taps(hid, f, w2, dims)
        finish(total, ext, f, stage, f, b2[...], length, frames, dims)
        pltpu.make_async_copy(stage.at[f], out.at[f], out_sem.at[f]).start()

    if comm:
        for i in range(2):
            @pl.when(exists(*sides[i]))
            def _():
                side_copy(i).wait_send()
        for f in range(frames):
            for i in range(3):
                @pl.when(exists(*onward[i]))
                def _():
                    onward_copy(i, f).wait_send()
    for f in range(frames):
        pltpu.make_async_copy(stage.at[f], out.at[f], out_sem.at[f]).wait()


def run_block(counts, comm, latent, tile_rows, kernel_one, bias_one, kernel_two, bias_two):
    frames, cap, cols, ch = latent.shape
    any_space = pl.BlockSpec(memory_space=pl.ANY)
    vmem = pl.BlockSpec(memory_space=pltpu.VMEM)
    return pl.pallas_call(
        functools.partial(block_kernel, counts, comm),
        out_shape=jax.ShapeDtypeStruct((frames, 2 * cap, 2 * cols, ch), BF16),
        in_specs=[pl.BlockSpec(memory_space=pltpu.SMEM), any_space, any_space, vmem, any_space, vmem],
        out_specs=any_space,
        scratch_shapes=[
            pltpu.VMEM((2 * frames, cap + 2, cols, ch), BF16),
            pltpu.VMEM((2 * frames, (cap + 2) * cols, ch), BF16),
            pltpu.VMEM((frames + 2, 4, cap + 1, 2, cols, ch), BF16),
            pltpu.VMEM(kernel_one.shape, BF16),
            pltpu.VMEM(kernel_two.shape, BF16),
            pltpu.VMEM((frames, cols, ch), BF16),
            pltpu.VMEM((frames, 2 * cap, 2 * cols, ch), BF16),
            pltpu.SemaphoreType.DMA((3,)),
            pltpu.SemaphoreType.DMA((frames,)),
            pltpu.SemaphoreType.DMA((2,)),
            pltpu.SemaphoreType.DMA((2,)),
            pltpu.SemaphoreType.DMA((3, frames)),
            pltpu.SemaphoreType.DMA((3, frames)),
        ],
        compiler_params=pltpu.CompilerParams(
            collective_id=0 if comm else None, has_side_effects=True, vmem_limit_bytes=56 * 2**20),
    )(tile_rows, latent, kernel_one, bias_one.reshape(1, ch), kernel_two, bias_two.reshape(1, ch))


def solution(mesh):
    counts = (mesh.shape["tm"], mesh.shape["tile"])
    in_specs = (P("tm", "tile", None, None), P(), P(), P(), P(), P())
    return jax.shard_map(functools.partial(run_block, counts, True), mesh=mesh, in_specs=in_specs,
                         out_specs=P("tm", "tile", None, None), check_vma=False)
```

time: 95.1 us -> 37.2 us (0.39)
  Pallas kernels: 0 us -> 34.8 us
  waiting for transfers between devices: 28.8 us -> 0 us
  local copies, waits for them, and re-layouts: 22.2 us -> 2.3 us
  matrix products: 18.1 us -> 0 us
  starting transfers between devices: 13.9 us -> 0 us
  other arithmetic: 8.73 us -> 0 us
  between operations: 2.8 us -> 0.01 us
    pallas_call x0 -> x1, Pallas kernels: none -> 34.8 us  [run_block(): pl.pallas_call(functools.partial(block_kernel, counts, comm), out_shape=j...]
    ppermute x6 -> x0, waiting for transfers between devices: 28.8 us -> none  [the longest x2 22.1 us: passed_along(): return lax.ppermute(block, axis, route)]
    conv_general_dilated x2 -> x0, matrix products: 18.1 us -> none  [convolve(): lax.conv_general_dilated(field[None], kernel, (1, 1, 1), ((0, 0), (0, 0),...]
    ppermute x6 -> x0, starting transfers between devices: 13.9 us -> none  [the longest x2 5.31 us: passed_along(): return lax.ppermute(block, axis, route)]
    select_n x5 -> x0, other arithmetic: 6.36 us -> none  [the longest x2 3.78 us: attach(): return jnp.where((row_ids == place)[None, :, None, None], below, extended)]
    convert_element_type x3 -> x0, local copies, waits for them, and re-layouts: 4.34 us -> none  [the longest x2 3.12 us: local(): residual = upsample(clean).astype(jnp.float32)]
    broadcast_in_dim x9 -> x0, local copies, waits for them, and re-layouts: 4.26 us -> none  [the longest x4 1.87 us: upsample(): return jnp.repeat(jnp.repeat(field, 2, axis=1), 2, axis=2)]
    unnamed x23 -> x1, local copies, waits for them, and re-layouts: 5.65 us -> 2.3 us
  transfers between devices with their start and end apart: 6 -> 0, of which waited for: 5 -> 0; matrix products, arithmetic and copies ran while one was open for 7% -> 0% of each run, Pallas kernels for 0% -> 0%
where the time goes in v1:
time: 37.2 us; the launch traced here: 37.1 us
  Pallas kernels  34.8 us (94%)
  local copies, waits for them, and re-layouts  2.3 us (6%)
    pallas_call x1, Pallas kernels, run_block(): pl.pallas_call(functools.partial(block_kernel, counts, comm), out_shape=j...  34.8 us
    unnamed x1, local copies, waits for them, and re-layouts  2.3 us

profile of v1, /device:TPU:112, one launch (start us, length us, event | category | flops | bytes accessed | tf_op | source)
XLA Modules:
  0.0 37.1 jit_solution(10372957466549937787)
XLA Ops:
  0.0 34.8 %shard_map.64 = bf16[4,8,64,256]{3,2,1,0:T(8,128)(2,1)} custom-call(s32[16]{0:T(128)} %tile_rows.1, bf16[4,4,32,256]{3,2,1,0:T(8,128)(2,1)} %lat.1, bf16[3,3,3,256,256]{4,3,2,1,0:T(8,128)(2,1)} %w1_hbm.1, f32[1,256]{1,0:T(1,128)} %bitcast.2, bf16[3,3,3,256,256]{4,3,2,1,0:T(8,128)(2,1)} %w2_hbm.1, f32[1,256]{1,0:T(1,128)} %bitcast.3), custom_call_target="tpu_custom_call" | custom-call | tf_op jit(solution)/shard_map/pallas_call | solution.py:225
  34.8 2.3 %copy.8 = bf16[4,8,64,256]{3,2,1,0:T(8,128)(2,1)} copy(bf16[4,8,64,256]{3,2,1,0:T(8,128)(2,1)} %shard_map.64) | data formatting | bytes 2097152

commit v2 on v1

v2 whole, which is shorter than its diff:
```python
import functools

import jax
import jax.numpy as jnp
from jax import lax
from jax.experimental import pallas as pl
from jax.experimental.pallas import tpu as pltpu
from jax.sharding import PartitionSpec as P

MESH = pl.DeviceIdType.MESH
F32, BF16 = jnp.float32, jnp.bfloat16


def shifted(value, by, cols):
    edge = lax.broadcasted_iota(jnp.int32, (8, value.shape[1]), 0)
    moved = pltpu.roll(value, by % value.shape[0], axis=0)
    pieces = []
    for start in range(0, value.shape[0], cols):
        if by > 0:
            pieces += [jnp.where(edge != 0, moved[start : start + 8], 0.0), moved[start + 8 : start + cols]]
        else:
            pieces += [moved[start : start + cols - 8],
                       jnp.where(edge != 7, moved[start + cols - 8 : start + cols], 0.0)]
    return jnp.concatenate(pieces, axis=0)


class Frames:
    def __init__(self, ref):
        self.ref = ref

    def __getitem__(self, k):
        return self.ref.at[k]


def spread(ext, hid, k, w1, half_bias, first, last, length, dims):
    cap, cols, ch = dims
    n = (cap + 1) * cols
    taps = jnp.concatenate([ext[k], ext[k + 1], ext[k + 2]], axis=1)
    upper, lower = taps[:n], taps[cols:]
    ends = jnp.concatenate([upper, lower], axis=1)
    even_rows, odd_rows = [], []
    for q in range(3):
        outer = jnp.concatenate([w1[:, 0, q].reshape(3 * ch, ch), w1[:, 2, q].reshape(3 * ch, ch)], axis=0)
        shared = jnp.dot(ends, outer, preferred_element_type=F32)
        centre = jnp.dot(taps, w1[:, 1, q].reshape(3 * ch, ch), preferred_element_type=F32)
        even_rows.append(shared + centre[cols:])
        odd_rows.append(shared + centre[:n])
    outside_odd = [first == 1] + [None] * cap
    outside_even = [jnp.logical_and(last == 1, length == j) if j else None for j in range(cap + 1)]
    for parity, (z, outside) in enumerate([(odd_rows, outside_odd), (even_rows, outside_even)]):
        even = shifted(z[0], 1, cols) + (z[1] + z[2])
        odd = (z[0] + z[1]) + shifted(z[2], -1, cols)
        pair = []
        for v in (even, odd):
            h = v * 0.5 + half_bias
            h = h + h * jnp.tanh(h)
            slots = [h[j * cols : (j + 1) * cols] for j in range(cap + 1)]
            slots = [x if o is None else jnp.where(o, 0.0, x) for x, o in zip(slots, outside)]
            pair.append(jnp.concatenate(slots, axis=0))
        even, odd = pair
        four = [shifted(odd, 1, cols), even, odd, shifted(even, -1, cols)]
        for variant, v in enumerate(four):
            hid[k][variant, :, parity] = v.astype(BF16).reshape(cap + 1, cols, ch)


def gather_taps(hid, f, w2, dims, taps=(2, 1, 0), rest=None):
    cap, cols, ch = dims
    total = None
    for a in taps:
        for p in range(3):
            for q in range(3):
                rows = hid[f + a][q : q + 2].reshape(2, 2 * cap + 2, cols, ch)[:, p : p + 2 * cap]
                part = jnp.dot(rows.reshape(4 * cap * cols, ch), w2[a, p, q], preferred_element_type=F32)
                total = part if total is None else total + part
    return total if rest is None else total + rest


def finish(total, ext, f, woven, stage, slot, bias, length, frames, dims):
    cap, cols, ch = dims
    total = total.reshape(2, 2 * cap, cols, ch)
    half = ch // 2
    for r in range(cap):
        residual = ext[frames + f, (r + 1) * cols : (r + 2) * cols].astype(F32) + bias
        for y in range(2 * r, 2 * r + 2):
            for c in range(2):
                value = total[c, y] + residual
                if r > 0:
                    value = jnp.where(r < length, value, 0.0)
                for h in range(2):
                    woven[slot, h, pl.ds(2 * cols * y + c, cols, stride=2)] = value[:, h * half : (h + 1) * half]
    for h in range(2):
        stage[slot, :, :, h * half : (h + 1) * half] = woven[slot, h].astype(BF16).reshape(2 * cap, 2 * cols, half)


def extend(rims, rows, ext, k, late, edges, dims):
    cap, cols, ch = dims
    has_up, has_down, has_prev, length, frames = edges
    above, below = (jnp.where(there, rims[i, k], jnp.zeros((cols, ch), BF16)) for i, there in enumerate((has_up, has_down)))
    for j in range(cap + 2):
        value = above if j == 0 else below if j == cap + 1 else rows[j - 1]
        if 2 <= j <= cap:
            value = jnp.where(length + 1 == j, below, value)
        place = slice(j * cols, (j + 1) * cols)
        if late:
            value = jnp.where(has_prev, value, ext[frames, place])
        ext[k, place] = value


def block_kernel(counts, comm, tile_rows, lat, w1_hbm, b1, w2_hbm, b2, out, mine, rims, halo, ext, hidden, w1, w2, rim, stage, woven,
                 load_sem, out_sem, side_send, side_recv, next_send, next_recv):
    n_tm, n_tile = counts
    frames, cap, cols, ch = lat.shape
    dims = (cap, cols, ch)
    group = lax.axis_index("tm") if comm else tile_rows[0] + 1
    tile = lax.axis_index("tile") if comm else tile_rows[1] + 3
    length = tile_rows[tile]
    first, last = (tile == 0).astype(jnp.int32), (tile == n_tile - 1).astype(jnp.int32)
    has_up, has_down, has_next, has_prev = tile > 0, tile < n_tile - 1, group < n_tm - 1, group > 0
    edges = (has_up, has_down, has_prev, length, frames)

    own = pltpu.make_async_copy(lat, mine, load_sem.at[0])
    own.start()
    load_one = pltpu.make_async_copy(w1_hbm, w1, load_sem.at[1])
    load_one.start()
    load_two = pltpu.make_async_copy(w2_hbm, w2, load_sem.at[2])
    load_two.start()

    sides = [(0, -1), (0, 1)]
    onward = [(1, 0), (1, -1), (1, 1)]

    def exists(dg, dt):
        ok = jnp.bool_(True)
        for step, there in ((dg, has_next if dg > 0 else has_prev), (dt, has_down if dt > 0 else has_up)):
            ok = jnp.logical_and(ok, there) if step else ok
        return ok

    def remote(source, target, send, recv, dg, dt):
        return pltpu.make_async_remote_copy(src_ref=source, dst_ref=target, send_sem=send, recv_sem=recv,
                                            device_id=(group + dg, tile + dt), device_id_type=MESH)

    def side_copy(i):
        source = (mine.at[:, 0], rim)[i]
        return remote(source, rims.at[1 - i, frames : 2 * frames], side_send.at[i], side_recv.at[i], *sides[i])

    def onward_copy(i, f):
        source, target = ((mine.at[f], halo.at[f]), (mine.at[f, 0], rims.at[1, f]), (rim.at[f], rims.at[0, f]))[i]
        return remote(source, target, next_send.at[i, f], next_recv.at[i, f], *onward[i])

    def lay(k):
        extend(rims, mine.at[k - frames], ext, k, False, edges, dims)

    def arrive(*late):
        for f in late:
            if comm:
                for i, (dg, dt) in enumerate(onward):
                    @pl.when(exists(-dg, -dt))
                    def _():
                        onward_copy(i, f).wait_recv()
            else:
                @pl.when(has_prev)
                def _():
                    pltpu.make_async_copy(lat.at[f], halo.at[f], next_recv.at[0, f]).wait()
        for f in late:
            extend(rims, halo.at[f], ext, f, True, edges, dims)

    if comm:
        barrier = pltpu.get_barrier_semaphore()
        for dg, dt in sides + onward:
            @pl.when(exists(-dg, -dt))
            def _():
                pl.semaphore_signal(barrier, inc=1, device_id=(group - dg, tile - dt), device_id_type=MESH)
    else:
        for f in range(frames):
            pltpu.make_async_copy(lat.at[f], halo.at[f], next_recv.at[0, f]).start()
    own.wait()
    for f in range(frames):
        rim[f] = mine[f, jnp.maximum(length - 1, 0)]
    if comm:
        pl.semaphore_wait(barrier, sum(exists(dg, dt).astype(jnp.int32) for dg, dt in sides + onward))
        for i in range(2):
            @pl.when(exists(*sides[i]))
            def _():
                side_copy(i).start()
        for f in reversed(range(frames)):
            for i in range(3):
                @pl.when(exists(*onward[i]))
                def _():
                    onward_copy(i, f).start()
        for i, (dg, dt) in enumerate(sides):
            @pl.when(exists(-dg, -dt))
            def _():
                side_copy(i).wait_recv()

    for k in range(frames, 2 * frames):
        lay(k)
    hid = Frames(hidden)
    args = (w1, b1[...] * 0.5, first, last, length, dims)

    def out_copy(f):
        return pltpu.make_async_copy(stage.at[f], out.at[f], out_sem.at[f])

    def last_step(total, f):
        finish(total, ext, f, woven, stage, f, b2[...], length, frames, dims)
        out_copy(f).start()

    load_one.wait()
    load_two.wait()
    spread(ext, hid, 5, *args)
    spread(ext, hid, 4, *args)

    def step(i, carry):
        f = frames - 1 - i
        arrive(f)
        spread(ext, hid, f, *args)
        last_step(gather_taps(hid, f, w2, dims), f)
        return carry

    lax.fori_loop(0, frames, step, 0)

    if comm:
        for i in range(2):
            @pl.when(exists(*sides[i]))
            def _():
                side_copy(i).wait_send()
        for f in range(frames):
            for i in range(3):
                @pl.when(exists(*onward[i]))
                def _():
                    onward_copy(i, f).wait_send()
    for f in range(frames):
        out_copy(f).wait()


def run_block(counts, comm, latent, tile_rows, kernel_one, bias_one, kernel_two, bias_two):
    frames, cap, cols, ch = latent.shape
    in_hbm = pl.BlockSpec(memory_space=pl.ANY)
    vmem = pl.BlockSpec(memory_space=pltpu.VMEM)
    smem = pl.BlockSpec(memory_space=pltpu.SMEM)
    dma = pltpu.SemaphoreType.DMA
    return pl.pallas_call(
        functools.partial(block_kernel, counts, comm),
        out_shape=jax.ShapeDtypeStruct((frames, 2 * cap, 2 * cols, ch), BF16),
        in_specs=[smem, in_hbm, in_hbm, vmem, in_hbm, vmem],
        out_specs=in_hbm,
        scratch_shapes=[
            pltpu.VMEM((frames, cap, cols, ch), BF16),
            pltpu.VMEM((2, 2 * frames, cols, ch), BF16),
            pltpu.VMEM((frames, cap, cols, ch), BF16),
            pltpu.VMEM((2 * frames, (cap + 2) * cols, ch), BF16),
            pltpu.VMEM((frames + 2, 4, cap + 1, 2, cols, ch), BF16),
            pltpu.VMEM(kernel_one.shape, BF16),
            pltpu.VMEM(kernel_two.shape, BF16),
            pltpu.VMEM((frames, cols, ch), BF16),
            pltpu.VMEM((frames, 2 * cap, 2 * cols, ch), BF16),
            pltpu.VMEM((frames, 2, 4 * cap * cols, ch // 2), F32),
            dma((3,)), dma((frames,)), dma((2,)), dma((2,)), dma((3, frames)), dma((3, frames)),
        ],
        compiler_params=pltpu.CompilerParams(
            collective_id=0 if comm else None, has_side_effects=True, vmem_limit_bytes=56 * 2**20),
    )(tile_rows, latent, kernel_one, bias_one.reshape(1, ch), kernel_two, bias_two.reshape(1, ch))


def solution(mesh):
    counts = (mesh.shape["tm"], mesh.shape["tile"])
    in_specs = (P("tm", "tile", None, None), P(), P(), P(), P(), P())
    return jax.shard_map(functools.partial(run_block, counts, True), mesh=mesh, in_specs=in_specs,
                         out_specs=P("tm", "tile", None, None), check_vma=False)
```

time: 37.2 us -> 26.9 us (0.72)
  Pallas kernels: 34.8 us -> 24.5 us
    pallas_call x1, Pallas kernels: 34.8 us -> 24.5 us  [run_block(): pl.pallas_call(functools.partial(block_kernel, counts, comm), out_shape=j...]
where the time goes in v2:
time: 26.9 us; the launch traced here: 26.8 us
  Pallas kernels  24.5 us (91%)
  local copies, waits for them, and re-layouts  2.3 us (9%)
    pallas_call x1, Pallas kernels, run_block(): pl.pallas_call(functools.partial(block_kernel, counts, comm), out_shape=j...  24.5 us
    unnamed x1, local copies, waits for them, and re-layouts  2.3 us

profile of v2, /device:TPU:112, one launch (start us, length us, event | category | flops | bytes accessed | tf_op | source)
XLA Modules:
  0.0 26.8 jit_solution(14820645106408309224)
XLA Ops:
  0.0 24.5 %shard_map.64 = bf16[4,8,64,256]{3,2,1,0:T(8,128)(2,1)} custom-call(s32[16]{0:T(128)} %tile_rows.1, bf16[4,4,32,256]{3,2,1,0:T(8,128)(2,1)} %lat.1, bf16[3,3,3,256,256]{4,3,2,1,0:T(8,128)(2,1)} %w1_hbm.1, f32[1,256]{1,0:T(1,128)} %bitcast.2, bf16[3,3,3,256,256]{4,3,2,1,0:T(8,128)(2,1)} %w2_hbm.1, f32[1,256]{1,0:T(1,128)} %bitcast.3), custom_call_target="tpu_custom_call" | custom-call | tf_op jit(solution)/shard_map/pallas_call | solution.py:240
  24.5 2.3 %copy.8 = bf16[4,8,64,256]{3,2,1,0:T(8,128)(2,1)} copy(bf16[4,8,64,256]{3,2,1,0:T(8,128)(2,1)} %shard_map.64) | data formatting | bytes 2097152

commit v3 on v2

--- a/solution.py
+++ b/solution.py
@@ -25,11 +25,11 @@
 
 
 class Frames:
-    def __init__(self, ref):
-        self.ref = ref
+    def __init__(self, ref, base):
+        self.ref, self.base = ref, base
 
     def __getitem__(self, k):
-        return self.ref.at[k]
+        return self.ref.at[k - self.base]
 
 
 def spread(ext, hid, k, w1, half_bias, first, last, length, dims):
@@ -106,15 +106,18 @@
         ext[k, place] = value
 
 
-def block_kernel(counts, comm, tile_rows, lat, w1_hbm, b1, w2_hbm, b2, out, mine, rims, halo, ext, hidden, w1, w2, rim, stage, woven,
-                 load_sem, out_sem, side_send, side_recv, next_send, next_recv):
+def place_of(comm, counts, tile_rows):
+    group = lax.axis_index("tm") if comm else tile_rows[0] + 1
+    tile = lax.axis_index("tile") if comm else tile_rows[1] + 3
+    return group, tile, tile_rows[tile], (tile == 0).astype(jnp.int32), (tile == counts[1] - 1).astype(jnp.int32)
+
+
+def early_kernel(counts, comm, tile_rows, lat, w1_hbm, b1, w2_hbm, b2, hid_late, ext, w1, w2, stage, partial, mine, rims, halo, rim, woven,
+                 load_sem, side_send, side_recv, next_send, next_recv):
     n_tm, n_tile = counts
     frames, cap, cols, ch = lat.shape
     dims = (cap, cols, ch)
-    group = lax.axis_index("tm") if comm else tile_rows[0] + 1
-    tile = lax.axis_index("tile") if comm else tile_rows[1] + 3
-    length = tile_rows[tile]
-    first, last = (tile == 0).astype(jnp.int32), (tile == n_tile - 1).astype(jnp.int32)
+    group, tile, length, first, last = place_of(comm, counts, tile_rows)
     has_up, has_down, has_next, has_prev = tile > 0, tile < n_tile - 1, group < n_tm - 1, group > 0
     edges = (has_up, has_down, has_prev, length, frames)
 
@@ -193,29 +196,27 @@
 
     for k in range(frames, 2 * frames):
         lay(k)
-    hid = Frames(hidden)
+    half = frames // 2
+    hid = Frames(hid_late, half)
     args = (w1, b1[...] * 0.5, first, last, length, dims)
-
-    def out_copy(f):
-        return pltpu.make_async_copy(stage.at[f], out.at[f], out_sem.at[f])
-
-    def last_step(total, f):
-        finish(total, ext, f, woven, stage, f, b2[...], length, frames, dims)
-        out_copy(f).start()
-
     load_one.wait()
     load_two.wait()
     spread(ext, hid, 5, *args)
     spread(ext, hid, 4, *args)
+    partial[...] = gather_taps(hid, frames - 1, w2, dims, (2, 1))
 
     def step(i, carry):
         f = frames - 1 - i
         arrive(f)
         spread(ext, hid, f, *args)
-        last_step(gather_taps(hid, f, w2, dims), f)
+        total = gather_taps(hid, f, w2, dims, (0,), partial[...])
+        coming = gather_taps(hid, f - 1, w2, dims, (2, 1))
+        finish(total, ext, f, woven, stage, f - half, b2[...], length, frames, dims)
+        partial[...] = coming
         return carry
 
-    lax.fori_loop(0, frames, step, 0)
+    lax.fori_loop(0, half, step, 0)
+    arrive(*reversed(range(half)))
 
     if comm:
         for i in range(2):
@@ -227,37 +228,81 @@
                 @pl.when(exists(*onward[i]))
                 def _():
                     onward_copy(i, f).wait_send()
+
+
+def late_kernel(counts, comm, tile_rows, hid_late, ext, w1, w2, stage_late, partial, b1, b2, out, hid_early, stage, woven, out_sem):
+    frames, cap, cols, ch = out.shape[0], out.shape[1] // 2, out.shape[2] // 2, out.shape[3]
+    dims = (cap, cols, ch)
+    half = frames // 2
+    _, _, length, first, last = place_of(comm, counts, tile_rows)
+    early, late = Frames(hid_early, 0), Frames(hid_late, half)
+    hid = [early[k] if k < half else late[k] for k in range(frames + 2)]
+    args = (w1, b1[...] * 0.5, first, last, length, dims)
+
+    def out_copy(f):
+        source = stage.at[f] if f < half else stage_late.at[f - half]
+        return pltpu.make_async_copy(source, out.at[f], out_sem.at[f])
+
+    for f in range(half, frames):
+        out_copy(f).start()
+    for f in reversed(range(half)):
+        spread(ext, hid, f, *args)
+    for f in reversed(range(half)):
+        taps = (0,) if f == half - 1 else (2, 1, 0)
+        total = gather_taps(hid, f, w2, dims, taps, partial[...] if f == half - 1 else None)
+        finish(total, ext, f, woven, stage, f, b2[...], length, frames, dims)
+        out_copy(f).start()
     for f in range(frames):
         out_copy(f).wait()
 
 
 def run_block(counts, comm, latent, tile_rows, kernel_one, bias_one, kernel_two, bias_two):
     frames, cap, cols, ch = latent.shape
+    half = frames // 2
     in_hbm = pl.BlockSpec(memory_space=pl.ANY)
     vmem = pl.BlockSpec(memory_space=pltpu.VMEM)
     smem = pl.BlockSpec(memory_space=pltpu.SMEM)
     dma = pltpu.SemaphoreType.DMA
-    return pl.pallas_call(
-        functools.partial(block_kernel, counts, comm),
-        out_shape=jax.ShapeDtypeStruct((frames, 2 * cap, 2 * cols, ch), BF16),
+    hidden = (4, cap + 1, 2, cols, ch)
+    frame = (2 * cap, 2 * cols, ch)
+    woven = (half, 2, 4 * cap * cols, ch // 2)
+    bias_one, bias_two = bias_one.reshape(1, ch), bias_two.reshape(1, ch)
+    kept = pl.pallas_call(
+        functools.partial(early_kernel, counts, comm),
+        out_shape=(
+            pltpu.VMEM((frames + 2 - half, *hidden), BF16),
+            pltpu.VMEM((2 * frames, (cap + 2) * cols, ch), BF16),
+            pltpu.VMEM(kernel_one.shape, BF16),
+            pltpu.VMEM(kernel_two.shape, BF16),
+            pltpu.VMEM((half, *frame), BF16),
+            pltpu.VMEM((4 * cap * cols, ch), F32),
+        ),
         in_specs=[smem, in_hbm, in_hbm, vmem, in_hbm, vmem],
-        out_specs=in_hbm,
+        out_specs=[vmem] * 6,
         scratch_shapes=[
             pltpu.VMEM((frames, cap, cols, ch), BF16),
             pltpu.VMEM((2, 2 * frames, cols, ch), BF16),
             pltpu.VMEM((frames, cap, cols, ch), BF16),
-            pltpu.VMEM((2 * frames, (cap + 2) * cols, ch), BF16),
-            pltpu.VMEM((frames + 2, 4, cap + 1, 2, cols, ch), BF16),
-            pltpu.VMEM(kernel_one.shape, BF16),
-            pltpu.VMEM(kernel_two.shape, BF16),
             pltpu.VMEM((frames, cols, ch), BF16),
-            pltpu.VMEM((frames, 2 * cap, 2 * cols, ch), BF16),
-            pltpu.VMEM((frames, 2, 4 * cap * cols, ch // 2), F32),
-            dma((3,)), dma((frames,)), dma((2,)), dma((2,)), dma((3, frames)), dma((3, frames)),
+            pltpu.VMEM(woven, F32),
+            dma((3,)), dma((2,)), dma((2,)), dma((3, frames)), dma((3, frames)),
         ],
         compiler_params=pltpu.CompilerParams(
-            collective_id=0 if comm else None, has_side_effects=True, vmem_limit_bytes=56 * 2**20),
-    )(tile_rows, latent, kernel_one, bias_one.reshape(1, ch), kernel_two, bias_two.reshape(1, ch))
+            collective_id=0 if comm else None, has_side_effects=True, vmem_limit_bytes=44 * 2**20),
+    )(tile_rows, latent, kernel_one, bias_one, kernel_two, bias_two)
+    return pl.pallas_call(
+        functools.partial(late_kernel, counts, comm),
+        out_shape=jax.ShapeDtypeStruct((frames, *frame), BF16),
+        in_specs=[smem] + [vmem] * 8,
+        out_specs=in_hbm,
+        scratch_shapes=[
+            pltpu.VMEM((half, *hidden), BF16),
+            pltpu.VMEM((half, *frame), BF16),
+            pltpu.VMEM(woven, F32),
+            dma((frames,)),
+        ],
+        compiler_params=pltpu.CompilerParams(vmem_limit_bytes=40 * 2**20),
+    )(tile_rows, *kept, bias_one, bias_two)
 
 
 def solution(mesh):

time: 26.9 us -> 23 us (0.86)
  local copies, waits for them, and re-layouts: 2.3 us -> 0.01 us
  Pallas kernels: 24.5 us -> 22.8 us
    unnamed x1 -> x6, local copies, waits for them, and re-layouts: 2.3 us -> 0.01 us
    pallas_call x1 -> x2, Pallas kernels: 24.5 us -> 22.8 us  [the longest x1 17.5 us: run_block(): pl.pallas_call(functools.partial(early_kernel, counts, comm), out_shape=(...]
where the time goes in v3:
time: 23 us; the launch traced here: 22.8 us
  Pallas kernels  22.8 us (99%)
    pallas_call x1, Pallas kernels, run_block(): pl.pallas_call(functools.partial(early_kernel, counts, comm), out_shape=(...  17.5 us
    pallas_call x1, Pallas kernels, run_block(): pl.pallas_call(functools.partial(late_kernel, counts, comm), out_shape=ja...  5.28 us

profile of v3, /device:TPU:112, one launch (start us, length us, event | category | flops | bytes accessed | tf_op | source)
XLA Modules:
  0.0 22.8 jit_solution(3201365215600754973)
XLA Ops:
  0.0 0.0 copy-start
  0.0 0.0 copy-start.1
  0.0 0.0 copy-start.2
  0.0 17.5 %shard_map.64 = (bf16[4,4,5,2,32,256]{5,4,3,2,1,0:T(8,128)(2,1)S(1)}, bf16[8,192,256]{2,1,0:T(8,128)(2,1)S(1)}, bf16[3,3,3,256,256]{4,3,2,1,0:T(8,128)(2,1)S(1)}...) custom-call(s32[16]{0:T(128)} %tile_rows.3, ...), custom_call_target="tpu_custom_call" | custom-call | tf_op jit(solution)/shard_map/pallas_call | solution.py:270
  17.5 0.0 copy-done
  17.5 0.0 copy-done.1
  17.5 0.0 copy-done.2
  17.5 5.3 %shard_map.65 = bf16[4,8,64,256]{3,2,1,0:T(8,128)(2,1)} custom-call(s32[16]{0:T(128)S(1)} %copy-done.2, bf16[4,4,5,2,32,256]{5,4,3,2,1,0:T(8,128)(2,1)S(1)} %get-tuple-element.11.hid_late, bf16[8,192,256]{2,1,0:T(8,128)(2,1)S(1)} %get-tuple-element.12.ext, bf16[3,3,3,256,256]{4,3,2,1,0:T(8,128)(2,1)S(1)} %get-tuple-element.13.w1, ...), custom_call_target="tpu_custom_call" | custom-call | tf_op jit(solution)/shard_map/pallas_call | solution.py:293
Async XLA Ops:
  0.0 17.5 %copy-start = (f32[256]{0:T(256)S(1)}, f32[256]{0:T(256)}, u32[]{:S(2)}) copy-start(f32[256]{0:T(256)} %param.9) | copy-start | bytes 3076
  0.0 17.5 %copy-start.1 = (f32[256]{0:T(256)S(1)}, f32[256]{0:T(256)}, u32[]{:S(2)}) copy-start(f32[256]{0:T(256)} %param.11) | copy-start | bytes 3076
  0.0 17.5 %copy-start.2 = (s32[16]{0:T(128)S(1)}, s32[16]{0:T(128)}, u32[]{:S(2)}) copy-start(s32[16]{0:T(128)} %tile_rows.3) | copy-start | bytes 196

commit v4 on v3

--- a/solution.py
+++ b/solution.py
@@ -32,19 +32,23 @@
         return self.ref.at[k - self.base]
 
 
-def spread(ext, hid, k, w1, half_bias, first, last, length, dims):
+def tap_products(taps, w1, dims, above=True):
     cap, cols, ch = dims
     n = (cap + 1) * cols
-    taps = jnp.concatenate([ext[k], ext[k + 1], ext[k + 2]], axis=1)
-    upper, lower = taps[:n], taps[cols:]
-    ends = jnp.concatenate([upper, lower], axis=1)
+    ends = jnp.concatenate([taps[:n], taps[cols:]], axis=1)
     even_rows, odd_rows = [], []
     for q in range(3):
         outer = jnp.concatenate([w1[:, 0, q].reshape(3 * ch, ch), w1[:, 2, q].reshape(3 * ch, ch)], axis=0)
         shared = jnp.dot(ends, outer, preferred_element_type=F32)
         centre = jnp.dot(taps, w1[:, 1, q].reshape(3 * ch, ch), preferred_element_type=F32)
         even_rows.append(shared + centre[cols:])
-        odd_rows.append(shared + centre[:n])
+        odd = shared + centre[:n] if above else jnp.concatenate([shared[:cols], shared[cols:] + centre[cols:n]], axis=0)
+        odd_rows.append(odd)
+    return even_rows, odd_rows
+
+
+def activate(even_rows, odd_rows, hid, k, half_bias, first, last, length, dims):
+    cap, cols, ch = dims
     outside_odd = [first == 1] + [None] * cap
     outside_even = [jnp.logical_and(last == 1, length == j) if j else None for j in range(cap + 1)]
     for parity, (z, outside) in enumerate([(odd_rows, outside_odd), (even_rows, outside_even)]):
@@ -63,33 +67,67 @@
             hid[k][variant, :, parity] = v.astype(BF16).reshape(cap + 1, cols, ch)
 
 
-def gather_taps(hid, f, w2, dims, taps=(2, 1, 0), rest=None):
+def frame_taps(ext, k):
+    return jnp.concatenate([ext[k], ext[k + 1], ext[k + 2]], axis=1)
+
+
+def spread(ext, hid, k, w1, half_bias, first, last, length, dims):
+    activate(*tap_products(frame_taps(ext, k), w1, dims), hid, k, half_bias, first, last, length, dims)
+
+
+def add_edges(before, edge, base, ks, hid, w1, half_bias, first, last, length, dims):
+    cap, cols, ch = dims
+    upper, lower = (
+        jnp.concatenate([jnp.concatenate([edge[i, k - base + a] for a in range(3)], axis=1) for k in ks], axis=0)
+        for i in range(2))
+    terms = []
+    for q in range(3):
+        weights = [w1[:, p, q].reshape(3 * ch, ch) for p in range(3)]
+        pairs = ((upper, 0), (upper, 1), (lower, 1), (lower, 2))
+        terms.append([jnp.dot(x, weights[p], preferred_element_type=F32) for x, p in pairs])
+    for i, k in enumerate(ks):
+        even_rows, odd_rows = [], []
+        for q in range(3):
+            at = slice(i * cols, (i + 1) * cols)
+            above_0, above_1, below_1, below_2 = (term[at] for term in terms[q])
+            for rows, own, top, bottom in ((even_rows, before[i, 0, q], above_0, below_1 + below_2),
+                                           (odd_rows, before[i, 1, q], above_0 + above_1, below_2)):
+                slots = [own[:cols] + top]
+                for j in range(1, cap + 1):
+                    slots.append(own[j * cols : (j + 1) * cols] + jnp.where(length == j, bottom, 0.0))
+                rows.append(jnp.concatenate(slots, axis=0))
+        activate(even_rows, odd_rows, hid, k, half_bias, first, last, length, dims)
+
+
+def gather_taps(hid, f, w2, dims, part, taps=(2, 1, 0), rest=None):
     cap, cols, ch = dims
     total = None
     for a in taps:
         for p in range(3):
             for q in range(3):
-                rows = hid[f + a][q : q + 2].reshape(2, 2 * cap + 2, cols, ch)[:, p : p + 2 * cap]
-                part = jnp.dot(rows.reshape(4 * cap * cols, ch), w2[a, p, q], preferred_element_type=F32)
-                total = part if total is None else total + part
+                start = p + part * cap
+                rows = hid[f + a][q : q + 2].reshape(2, 2 * cap + 2, cols, ch)[:, start : start + cap]
+                term = jnp.dot(rows.reshape(2 * cap * cols, ch), w2[a, p, q], preferred_element_type=F32)
+                total = term if total is None else total + term
     return total if rest is None else total + rest
 
 
-def finish(total, ext, f, woven, stage, slot, bias, length, frames, dims):
-    cap, cols, ch = dims
-    total = total.reshape(2, 2 * cap, cols, ch)
+def finish(total, ext, f, woven, stage, slot, bias, length, frames, dims, part):
+    cap, cols, ch = dims
+    total = total.reshape(2, cap, cols, ch)
     half = ch // 2
-    for r in range(cap):
+    for r in range(part * cap // 2, (part + 1) * cap // 2):
         residual = ext[frames + f, (r + 1) * cols : (r + 2) * cols].astype(F32) + bias
         for y in range(2 * r, 2 * r + 2):
             for c in range(2):
-                value = total[c, y] + residual
+                value = total[c, y - part * cap] + residual
                 if r > 0:
                     value = jnp.where(r < length, value, 0.0)
                 for h in range(2):
                     woven[slot, h, pl.ds(2 * cols * y + c, cols, stride=2)] = value[:, h * half : (h + 1) * half]
+    rows, flat = slice(part * cap, (part + 1) * cap), slice(2 * cols * part * cap, 2 * cols * (part + 1) * cap)
     for h in range(2):
-        stage[slot, :, :, h * half : (h + 1) * half] = woven[slot, h].astype(BF16).reshape(2 * cap, 2 * cols, half)
+        stage[slot, rows, :, h * half : (h + 1) * half] = woven[slot, h, flat].astype(BF16).reshape(cap, 2 * cols, half)
 
 
 def extend(rims, rows, ext, k, late, edges, dims):
@@ -112,7 +150,7 @@
     return group, tile, tile_rows[tile], (tile == 0).astype(jnp.int32), (tile == counts[1] - 1).astype(jnp.int32)
 
 
-def early_kernel(counts, comm, tile_rows, lat, w1_hbm, b1, w2_hbm, b2, hid_late, ext, w1, w2, stage, partial, mine, rims, halo, rim, woven,
+def early_kernel(counts, comm, tile_rows, lat, w1_hbm, b1, w2_hbm, b2, hid_late, ext, w1, w2, stage, partial, mine, rims, halo, rim, woven, edge, before,
                  load_sem, side_send, side_recv, next_send, next_recv):
     n_tm, n_tile = counts
     frames, cap, cols, ch = lat.shape
@@ -189,30 +227,46 @@
                 @pl.when(exists(*onward[i]))
                 def _():
                     onward_copy(i, f).start()
+
+    half = frames // 2
+    hid = Frames(hid_late, half)
+    args = (w1, b1[...] * 0.5, first, last, length, dims)
+
+    for k in range(frames):
+        for j in range(cap + 2):
+            value = jnp.zeros((cols, ch), BF16)
+            if 1 <= j <= cap:
+                value = mine[k, j - 1] if j == 1 else jnp.where(j <= length, mine[k, j - 1], value)
+            ext[frames + k, j * cols : (j + 1) * cols] = value
+    load_one.wait()
+    alone = (frames + 1, frames)
+    for i, k in enumerate(alone):
+        for parity, rows in enumerate(tap_products(frame_taps(ext, k), w1, dims, False)):
+            for q in range(3):
+                before[i, parity, q] = rows[q]
+    if comm:
         for i, (dg, dt) in enumerate(sides):
             @pl.when(exists(-dg, -dt))
             def _():
                 side_copy(i).wait_recv()
-
     for k in range(frames, 2 * frames):
         lay(k)
-    half = frames // 2
-    hid = Frames(hid_late, half)
-    args = (w1, b1[...] * 0.5, first, last, length, dims)
-    load_one.wait()
+    for i, there in enumerate((has_up, has_down)):
+        for k in range(frames):
+            edge[i, k] = jnp.where(there, rims[i, frames + k], jnp.zeros((cols, ch), BF16))
     load_two.wait()
-    spread(ext, hid, 5, *args)
-    spread(ext, hid, 4, *args)
-    partial[...] = gather_taps(hid, frames - 1, w2, dims, (2, 1))
+    add_edges(before, edge, frames, alone, hid, *args)
+    for part in range(2):
+        partial[part] = gather_taps(hid, frames - 1, w2, dims, part, (2, 1))
 
     def step(i, carry):
         f = frames - 1 - i
         arrive(f)
         spread(ext, hid, f, *args)
-        total = gather_taps(hid, f, w2, dims, (0,), partial[...])
-        coming = gather_taps(hid, f - 1, w2, dims, (2, 1))
-        finish(total, ext, f, woven, stage, f - half, b2[...], length, frames, dims)
-        partial[...] = coming
+        for part in range(2):
+            total = gather_taps(hid, f, w2, dims, part, (0,), partial[part])
+            finish(total, ext, f, woven, stage, f - half, b2[...], length, frames, dims, part)
+            partial[part] = gather_taps(hid, f - 1, w2, dims, part, (2, 1))
         return carry
 
     lax.fori_loop(0, half, step, 0)
@@ -240,20 +294,27 @@
     args = (w1, b1[...] * 0.5, first, last, length, dims)
 
     def out_copy(f):
-        source = stage.at[f] if f < half else stage_late.at[f - half]
-        return pltpu.make_async_copy(source, out.at[f], out_sem.at[f])
+        return pltpu.make_async_copy(stage_late.at[f - half], out.at[f], out_sem.at[f, 0])
+
+    def half_copy(f, part):
+        rows = slice(part * cap, (part + 1) * cap)
+        return pltpu.make_async_copy(stage.at[f, rows], out.at[f, rows], out_sem.at[f, part])
 
     for f in range(half, frames):
         out_copy(f).start()
     for f in reversed(range(half)):
         spread(ext, hid, f, *args)
     for f in reversed(range(half)):
-        taps = (0,) if f == half - 1 else (2, 1, 0)
-        total = gather_taps(hid, f, w2, dims, taps, partial[...] if f == half - 1 else None)
-        finish(total, ext, f, woven, stage, f, b2[...], length, frames, dims)
-        out_copy(f).start()
-    for f in range(frames):
+        for part in range(2):
+            taps, rest = ((0,), partial[part]) if f == half - 1 else ((2, 1, 0), None)
+            total = gather_taps(hid, f, w2, dims, part, taps, rest)
+            finish(total, ext, f, woven, stage, f, b2[...], length, frames, dims, part)
+            half_copy(f, part).start()
+    for f in range(half, frames):
         out_copy(f).wait()
+    for f in range(half):
+        for part in range(2):
+            half_copy(f, part).wait()
 
 
 def run_block(counts, comm, latent, tile_rows, kernel_one, bias_one, kernel_two, bias_two):
@@ -275,7 +336,7 @@
             pltpu.VMEM(kernel_one.shape, BF16),
             pltpu.VMEM(kernel_two.shape, BF16),
             pltpu.VMEM((half, *frame), BF16),
-            pltpu.VMEM((4 * cap * cols, ch), F32),
+            pltpu.VMEM((2, 2 * cap * cols, ch), F32),
         ),
         in_specs=[smem, in_hbm, in_hbm, vmem, in_hbm, vmem],
         out_specs=[vmem] * 6,
@@ -285,6 +346,8 @@
             pltpu.VMEM((frames, cap, cols, ch), BF16),
             pltpu.VMEM((frames, cols, ch), BF16),
             pltpu.VMEM(woven, F32),
+            pltpu.VMEM((2, frames, cols, ch), BF16),
+            pltpu.VMEM((2, 2, 3, (cap + 1) * cols, ch), F32),
             dma((3,)), dma((2,)), dma((2,)), dma((3, frames)), dma((3, frames)),
         ],
         compiler_params=pltpu.CompilerParams(
@@ -299,7 +362,7 @@
             pltpu.VMEM((half, *hidden), BF16),
             pltpu.VMEM((half, *frame), BF16),
             pltpu.VMEM(woven, F32),
-            dma((frames,)),
+            dma((frames, 2)),
         ],
         compiler_params=pltpu.CompilerParams(vmem_limit_bytes=40 * 2**20),
     )(tile_rows, *kept, bias_one, bias_two)

time: 23 us -> 23.1 us (level)
  no operation moved by 1% of the time
where the time goes in v4:
time: 23.1 us
  Pallas kernels  23 us (100%)
    pallas_call x1, Pallas kernels, run_block(): pl.pallas_call(functools.partial(early_kernel, counts, comm), out_shape=(...  17.5 us
    pallas_call x1, Pallas kernels, run_block(): pl.pallas_call(functools.partial(late_kernel, counts, comm), out_shape=ja...  5.49 us

profile of v4, /device:TPU:112, one launch (start us, length us, event | category | flops | bytes accessed | tf_op | source)
XLA Modules:
  0.0 23.1 jit_solution(11852955974364562719)
XLA Ops:
  0.0 0.0 copy-start
  0.0 0.0 copy-start.1
  0.0 0.0 copy-start.2
  0.0 17.5 %shard_map.64 = (bf16[4,4,5,2,32,256]{5,4,3,2,1,0:T(8,128)(2,1)S(1)}, bf16[8,192,256]{2,1,0:T(8,128)(2,1)S(1)}, bf16[3,3,3,256,256]{4,3,2,1,0:T(8,128)(2,1)S(1)}...) custom-call(s32[16]{0:T(128)} %tile_rows.3, ...), custom_call_target="tpu_custom_call" | custom-call | tf_op jit(solution)/shard_map/pallas_call | solution.py:331
  17.5 0.0 copy-done
  17.5 0.0 copy-done.1
  17.6 0.0 copy-done.2
  17.6 5.5 %shard_map.65 = bf16[4,8,64,256]{3,2,1,0:T(8,128)(2,1)} custom-call(s32[16]{0:T(128)S(1)} %copy-done.2, bf16[4,4,5,2,32,256]{5,4,3,2,1,0:T(8,128)(2,1)S(1)} %get-tuple-element.11.hid_late, bf16[8,192,256]{2,1,0:T(8,128)(2,1)S(1)} %get-tuple-element.12.ext, bf16[3,3,3,256,256]{4,3,2,1,0:T(8,128)(2,1)S(1)} %get-tuple-element.13.w1, ...), custom_call_target="tpu_custom_call" | custom-call | tf_op jit(solution)/shard_map/pallas_call | solution.py:356
Async XLA Ops:
  0.0 17.5 %copy-start = (f32[256]{0:T(256)S(1)}, f32[256]{0:T(256)}, u32[]{:S(2)}) copy-start(f32[256]{0:T(256)} %param.9) | copy-start | bytes 3076
  0.0 17.5 %copy-start.1 = (f32[256]{0:T(256)S(1)}, f32[256]{0:T(256)}, u32[]{:S(2)}) copy-start(f32[256]{0:T(256)} %param.11) | copy-start | bytes 3076
  0.0 17.6 %copy-start.2 = (s32[16]{0:T(128)S(1)}, s32[16]{0:T(128)}, u32[]{:S(2)}) copy-start(s32[16]{0:T(128)} %tile_rows.3) | copy-start | bytes 196
